TPU v7x, 256 devices: a whole 4x4x8 slice. The times are simulated.
256 devices in a mesh: bulk: 16 (over z, core), wide: 16 (over y, x).
Axes of the slice: x: 4, y: 4, z: 8, core: 2. Of those that a mesh axis runs over, the one named last changes fastest.
Arguments:
- wavefunction: float32 [16384, 512], P('wide'), may hold values from -6 to 6
- env_blocks: float32 [256, 2048, 1024], P('bulk', 'wide'), may hold values from -0.1875 to 0.1875
- right_env: float32 [32, 512, 512], P('bulk'), may hold values from -0.0625 to 0.0625
- tile_sector: int32 [128], replicated, may hold values from 0 to 31, never falling along the last dimension, each value on 1 to 8 neighbouring positions
- term_charge: int32 [32], replicated, may hold values from -1 to 1
- block_home: int32 [16, 16], replicated, may hold values from 0 to 15, as said below
Outputs:
- applied: float32 [16384, 512], P('wide', 'bulk')
Inputs may be any that keep to these rules, and one draw needn't show every extreme that they name: `tile_sector`: never falls; each sector 0 to 31 covers 1 to 8 whole tiles, one exactly 8. `term_charge`: each MPO term raises, keeps or lowers the left quantum number by one. For each pair index k the column block_home[:, k] is a permutation of the bulk indices, so every device stores exactly one block of each k; at most 2 blocks of one term owner lie on one device, and some device holds 2 of them.
All inputs are finite; a program needn't handle non-finite values.
Results may differ from a plain program's by a relative error of at most 0.0003.
Values sent between devices are 32-bit elements; how exact they have to be, the bound alone decides.
No kernel may reach another device: no remote copies, remote signals or barrier semaphores. Data moves between devices by JAX's collectives and lax.ppermute only.
A program may use at most 192 MiB of HBM per device.

v0:
```python
import jax
import jax.numpy as jnp
from jax import lax
from jax.sharding import PartitionSpec as P

TILE = 128
NW_DEV = 2
SLOT = 2
TILE_DEV = 8
SRC = 1024
PAIRS = 16
REACH = 2


precise = lax.Precision.HIGHEST


def from_behind(value, axis, steps):
    count = lax.axis_size(axis)
    initial, last = (max(0, -steps), min(count, count - steps))
    return lax.ppermute(value, axis, [(source, source + steps) for source in range(initial, last)])


def neighbour(panel, offset):
    return from_behind(panel, "wide", offset)


def window_plan(tile_sector, term_charge, tiles_of, terms_of):
    count_tiles = tile_sector.shape[0]
    labels = jnp.arange(count_tiles, dtype=jnp.int32)
    starts = jnp.sum((tile_sector[None, :] < labels[:, None]).astype(jnp.int32), axis=1)
    widths = jnp.sum((tile_sector[None, :] == labels[:, None]).astype(jnp.int32), axis=1)
    sectors = tile_sector[count_tiles - 1] + 1
    source = tile_sector[tiles_of] + term_charge[terms_of]
    usable = (source >= 0) & (source < sectors)
    clipped = jnp.clip(source, 0, count_tiles - 1)
    return (starts[clipped], jnp.where(usable, widths[clipped] * TILE, 0))


def on_device(wavefunction, env_blocks, right_env, tile_sector, term_charge, block_home):
    home_count = lax.axis_size("bulk")
    owner_index = lax.axis_index("bulk")
    column = lax.axis_index("wide")
    below_rows = [neighbour(wavefunction, offset) for offset in range(REACH, 0, -1)]
    above_rows = [neighbour(wavefunction, -offset) for offset in range(1, REACH + 1)]
    extended = jnp.concatenate(below_rows + [wavefunction] + above_rows, axis=0)
    base_tile = (column - REACH) * TILE_DEV
    window_rows = jnp.arange(SRC, dtype=jnp.int32)
    pair_ids = jnp.arange(PAIRS, dtype=jnp.int32)
    tile_local = pair_ids // NW_DEV
    term_local = pair_ids % NW_DEV
    my_tiles = column * TILE_DEV + tile_local
    earlier = pair_ids[None, :] < pair_ids[:, None]
    home_ids = jnp.arange(home_count, dtype=jnp.int32)
    stored_dest = jnp.sum(home_ids[:, None] * (block_home == owner_index).astype(jnp.int32), axis=0)
    stored_slot = jnp.sum(
        (earlier & (stored_dest[None, :] == stored_dest[:, None])).astype(jnp.int32), axis=1
    )
    matched = (stored_dest[None, None, :] == home_ids[:, None, None]) & (
        stored_slot[None, None, :] == jnp.arange(SLOT, dtype=jnp.int32)[None, :, None]
    )
    pick_index = jnp.sum(pair_ids[None, None, :] * matched.astype(jnp.int32), axis=2)
    filled = jnp.any(matched, axis=2)
    home_of = block_home[owner_index]
    slot_of = jnp.sum((earlier & (home_of[None, :] == home_of[:, None])).astype(jnp.int32), axis=1)
    arrival = home_of * SLOT + slot_of

    def contract_left(operands):
        env_block, start_row, live_rows = operands
        window = lax.dynamic_slice(extended, (start_row, jnp.int32(0)), (SRC, extended.shape[1]))
        window = jnp.where((window_rows < live_rows)[:, None], window, 0.0)
        return jnp.dot(env_block, window, precision=precise, preferred_element_type=jnp.float32)

    packed = jnp.take(env_blocks, pick_index.reshape(-1), axis=0).reshape(
        (home_count, SLOT) + env_blocks.shape[1:]
    )
    arrived = lax.all_to_all(
        jnp.where(filled[:, :, None, None], packed, 0.0),
        "bulk",
        split_axis=0,
        concat_axis=0,
        tiled=True,
    )
    blocks = arrived.reshape((home_count * SLOT,) + env_blocks.shape[1:])[arrival]
    my_terms = owner_index * NW_DEV + term_local
    first_tile, live_rows = window_plan(tile_sector, term_charge, my_tiles, my_terms)
    first_row = (first_tile - base_tile) * TILE
    left_parts = lax.map(contract_left, (blocks, first_row, live_rows))

    def contract_right(operands):
        left_part, term_index = operands
        return jnp.dot(
            left_part, right_env[term_index], precision=precise, preferred_element_type=jnp.float32
        )

    term_parts = lax.map(contract_right, (left_parts, term_local))
    summed = jnp.sum(term_parts.reshape(TILE_DEV, NW_DEV, TILE, term_parts.shape[2]), axis=1)
    summed = summed.reshape(TILE_DEV * TILE, term_parts.shape[2])
    return lax.psum_scatter(summed, "bulk", scatter_dimension=1, tiled=True)


def solution(mesh):
    return jax.shard_map(
        on_device,
        mesh=mesh,
        in_specs=(P("wide", None), P("bulk", "wide", None), P("bulk", None, None), P(), P(), P()),
        out_specs=P("wide", "bulk"),
        check_vma=False,
    )
```

profile of v0, /device:TPU:29, one launch (start us, length us, event | category | flops | bytes accessed | tf_op | source)
XLA Modules:
  0.0 696.1 jit_solution(16264479814748081253)
XLA Ops:
  10.2 11.5 %gather_fusion = f32[32,128,1024]{2,1,0:T(8,128)} fusion(f32[16,128,1024]{2,1,0:T(8,128)} %param.11, s32[1024]{0:T(1024)S(1)} %get-tuple-element.110), kind=kCustom, calls=%fused_computation | custom fusion | bytes 33554560 | tf_op jit(solution)/shard_map/jit(_take)/gather | solution.py:74
  21.7 12.6 %select_select_fusion = f32[16,2,128,1024]{3,2,1,0:T(8,128)} fusion(f32[16,2,128,1024]{3,2,1,0:T(8,128)} %bitcast.62, pred[16,2]{1,0:T(8,128)(4,1)S(1)} %copy.9, pred[16,2]{1,0:T(8,128)(4,1)S(1)} %copy.8), kind=kLoop, calls=%fused_computation.26 | loop fusion | flops 8388608 | bytes 33554496 | tf_op jit(solution)/shard_map/jit(_where)/select_n | solution.py:78
  34.2 9.3 %all-to-all-start = ((f32[16,2,128,1024]{3,2,1,0:T(8,128)}), f32[16,2,128,1024]{3,2,1,0:T(8,128)}, u32[]{:S(2)}, u32[]{:S(2)}) async-start(f32[16,2,128,1024]{3,2,1,0:T(8,128)} %select_select_fusion), calls=%async_computation | async-start | bytes 33554432 | tf_op jit(solution)/shard_map/all_to_all | solution.py:77
  47.7 3.7 collective-permute-start.2
  51.4 7.6 %collective-permute-start.3 = (f32[1024,512]{1,0:T(8,128)S(1)}, f32[1024,512]{1,0:T(8,128)}, u32[]{:S(2)}, u32[]{:S(2)}) collective-permute-start(f32[1024,512]{1,0:T(8,128)S(1)} %copy-done.4), channel_id=1, source_target_pairs={{2,0},{3,1},{4,2},{5,3},{6,4},{7,5},{8,6},{9,7},{10,8},{11,9},{12,... | collective-permute-start | bytes 6291464 | tf_op jit(solution)/shard_map/ppermute | solution.py:21
  63.5 30.7 %collective-permute-done = f32[1024,512]{1,0:T(8,128)} collective-permute-done((f32[1024,512]{1,0:T(8,128)S(1)}, f32[1024,512]{1,0:T(8,128)}, u32[]{:S(2)}, u32[]{:S(2)}) %collective-permute-start) | collective-permute-done | bytes 2097184 | tf_op jit(solution)/shard_map/ppermute | solution.py:21
  94.2 3.1 constant_dynamic-update-slice_fusion.4
  97.2 42.9 %collective-permute-done.1 = f32[1024,512]{1,0:T(8,128)} collective-permute-done((f32[1024,512]{1,0:T(8,128)S(1)}, f32[1024,512]{1,0:T(8,128)}, u32[]{:S(2)}, u32[]{:S(2)}) %collective-permute-start.1) | collective-permute-done | bytes 2097184 | tf_op jit(solution)/shard_map/ppermute | solution.py:21
  140.1 3.1 constant_dynamic-update-slice_fusion.3
  144.7 3.1 constant_dynamic-update-slice_fusion.1
  147.8 3.1 constant_dynamic-update-slice_fusion
  150.9 255.7 %all-to-all-done = f32[16,2,128,1024]{3,2,1,0:T(8,128)} async-done(((f32[16,2,128,1024]{3,2,1,0:T(8,128)}), f32[16,2,128,1024]{3,2,1,0:T(8,128)}, u32[]{:S(2)}, u32[]{:S(2)}) %all-to-all-start) | async-done | bytes 16777248 | tf_op jit(solution)/shard_map/all_to_all | solution.py:77
  406.6 10.1 %gather_fusion.1 = f32[16,128,1024]{2,1,0:T(8,128)} fusion(f32[32,128,1024]{2,1,0:T(8,128)} %bitcast.6, s32[1024]{0:T(1024)S(1)} %pad_clamp_fusion.3), kind=kCustom, calls=%fused_computation.1 | custom fusion | bytes 16777280 | tf_op jit(solution)/shard_map/gather | solution.py:84
  419.2 128.9 %while.22 = (s32[]{:T(128)}, f32[16,128,512]{2,1,0:T(8,128)}, f32[16,128,1024]{2,1,0:T(8,128)}, s32[16]{0:T(128)S(1)}, s32[16]{0:T(128)S(1)}, /*index=5*/f32[5120,512]{1,0:T(8,128)}, s32[]{:T(128)}, s32[]{:T(128)}, s32[]{:T(128)}) while((s32[]{:T(128)}, f32[16,128,512]{2,1,0:T(8,128)}, f32[16,128,1024]{2,1,0:T(8,128)}, ...), condition=%wide.region_8.9_spmd.clone, body=%wide.region_7.8_spmd.clone.sunk | while | flops 805831680 | bytes 2886815 | solution.py:88
  423.2 4.0 fusion.45
  431.2 4.0 fusion.45
  439.3 4.1 fusion.45
  447.4 4.1 fusion.45
  455.4 4.0 fusion.45
  463.5 4.1 fusion.45
  471.5 4.1 fusion.45
  479.6 4.0 fusion.45
  487.6 4.1 fusion.45
  495.7 4.1 fusion.45
  503.8 4.1 fusion.45
  511.8 4.0 fusion.45
  519.9 4.0 fusion.45
  527.9 4.0 fusion.45
  535.9 4.0 fusion.45
  544.0 4.1 fusion.45
  550.5 77.2 %while.21 = (s32[]{:T(128)}, f32[16,128,512]{2,1,0:T(8,128)}, f32[16,128,512]{2,1,0:T(8,128)}, s32[16]{0:T(128)S(1)}, f32[2,512,512]{2,1,0:T(8,128)S(1)}, /*index=5*/s32[]{:T(128)}, s32[]{:T(128)}, s32[]{:T(128)}) while((s32[]{:T(128)}, f32[16,128,512]{2,1,0:T(8,128)}, f32[16,128,512]{2,1,0:T(8,128)}, s32[16]{0:T(128)S(1)}, ...), condition=%wide.region_10.11_spmd, body=%wide.region_9.10_spmd.sunk | while | flops 402653184 | bytes 1574023 | solution.py:96
  632.6 56.7 %reduce-scatter.2.cloned.1.call-done = f32[1024,32]{0,1:T(8,128)} async-done(((f32[1024,512]{0,1:T(8,128)}), f32[1024,32]{0,1:T(8,128)}) %reduce-scatter.2.cloned.1.call-update) | async-done | bytes 131088 | tf_op jit(solution)/shard_map/reduce_scatter | solution.py:99
  (132 shorter events, 101.9 us)
Async XLA Ops:
  6.5 1.6 copy-start
  34.2 9.3 %copy-start.4 = (f32[1024,512]{1,0:T(8,128)S(1)}, f32[1024,512]{1,0:T(8,128)}, u32[]{:S(2)}) copy-start(f32[1024,512]{1,0:T(8,128)} %param.10) | copy-start | bytes 6291460
  34.2 24.8 %copy-start.2 = (s32[128]{0:T(128)S(1)}, s32[128]{0:T(128)}, u32[]{:S(2)}) copy-start(s32[128]{0:T(128)} %param.13) | copy-start | bytes 1540
  34.2 372.4 %all-to-all-start = ((f32[16,2,128,1024]{3,2,1,0:T(8,128)}), f32[16,2,128,1024]{3,2,1,0:T(8,128)}, u32[]{:S(2)}, u32[]{:S(2)}) async-start(f32[16,2,128,1024]{3,2,1,0:T(8,128)} %select_select_fusion), calls=%async_computation | async-start | bytes 33554432 | tf_op jit(solution)/shard_map/all_to_all | solution.py:77
  43.5 645.7 %reduce-scatter.2.cloned.1.call-start = ((), (), s32[]{:S(2)}) async-start(), calls=%async_computation.2 | async-start | bytes 2228224 | tf_op jit(solution)/shard_map/reduce_scatter | solution.py:99
  43.6 50.6 %collective-permute-start = (f32[1024,512]{1,0:T(8,128)S(1)}, f32[1024,512]{1,0:T(8,128)}, u32[]{:S(2)}, u32[]{:S(2)}) collective-permute-start(f32[1024,512]{1,0:T(8,128)S(1)} %copy-done.4), channel_id=1, source_target_pairs={{0,2},{1,3},{2,4},{3,5},{4,6},{5,7},{6,8},{7,9},{8,10},{9,11},{10,... | collective-permute-start | bytes 6291464 | tf_op jit(solution)/shard_map/ppermute | solution.py:21
  44.9 95.2 %collective-permute-start.1 = (f32[1024,512]{1,0:T(8,128)S(1)}, f32[1024,512]{1,0:T(8,128)}, u32[]{:S(2)}, u32[]{:S(2)}) collective-permute-start(f32[1024,512]{1,0:T(8,128)S(1)} %copy-done.4), channel_id=1, source_target_pairs={{0,1},{1,2},{2,3},{3,4},{4,5},{5,6},{6,7},{7,8},{8,9},{9,10},{10,1... | collective-permute-start | bytes 6291464 | tf_op jit(solution)/shard_map/ppermute | solution.py:21
  47.7 97.0 %collective-permute-start.2 = (f32[1024,512]{1,0:T(8,128)S(1)}, f32[1024,512]{1,0:T(8,128)}, u32[]{:S(2)}, u32[]{:S(2)}) collective-permute-start(f32[1024,512]{1,0:T(8,128)S(1)} %copy-done.4), channel_id=1, source_target_pairs={{1,0},{2,1},{3,2},{4,3},{5,4},{6,5},{7,6},{8,7},{9,8},{10,9},{11,1... | collective-permute-start | bytes 6291464 | tf_op jit(solution)/shard_map/ppermute | solution.py:21
  51.4 96.4 %collective-permute-start.3 = (f32[1024,512]{1,0:T(8,128)S(1)}, f32[1024,512]{1,0:T(8,128)}, u32[]{:S(2)}, u32[]{:S(2)}) collective-permute-start(f32[1024,512]{1,0:T(8,128)S(1)} %copy-done.4), channel_id=1, source_target_pairs={{2,0},{3,1},{4,2},{5,3},{6,4},{7,5},{8,6},{9,7},{10,8},{11,9},{12,... | collective-permute-start | bytes 6291464 | tf_op jit(solution)/shard_map/ppermute | solution.py:21
  548.0 2.5 copy-start.3
  627.7 61.5 %copy-start.1 = (s32[32]{0:T(128)S(1)}, s32[32]{0:T(128)}, u32[]{:S(2)}) copy-start(s32[32]{0:T(128)} %param.14) | copy-start | bytes 388
Sparse Core Ops, SparseCore 0:
  632.7 56.4 reduce-scatter.1
where the time goes:
time: 702 us; the launch traced here: 696 us
  waiting for transfers between devices  386 us (55%)
  matrix products  103 us (15%)
  local copies, waits for them, and re-layouts  77.5 us (11%)
  loops' own time  62.2 us (9%)
  other arithmetic  28.6 us (4%)
  starting transfers between devices  24.8 us (4%)
  between operations  14.2 us (2%)
    all_to_all x1, waiting for transfers between devices, on_device(): lax.all_to_all(jnp.where(filled[:, :, None, None], packed, 0.0), 'bulk',...  256 us
    ppermute x4, waiting for transfers between devices, from_behind(): lax.ppermute(value, axis, [(source, source + steps) for source in range(i...  73.6 us
    dot_general x16, matrix products, contract_left(): jnp.dot(env_block, window, precision=precise, preferred_element_type=jnp....  64.8 us
    reduce_scatter x1, waiting for transfers between devices, on_device(): return lax.psum_scatter(summed, 'bulk', scatter_dimension=1, tiled=True)  56.7 us
    dot_general x16, matrix products, contract_right(): jnp.dot(left_part, right_env[term_index], precision=precise, preferred_el...  38.1 us
    another operation x1, loops' own time, on_device(): left_parts = lax.map(contract_left, (blocks, first_row, live_rows))  32.5 us
    dynamic_slice x48, local copies, waits for them, and re-layouts, on_device(): left_parts = lax.map(contract_left, (blocks, first_row, live_rows))  30.2 us
    another operation x1, loops' own time, on_device(): term_parts = lax.map(contract_right, (left_parts, term_local))  29.7 us
  transfers between devices with their start and end apart: 6, of which 4 were waited for; matrix products, arithmetic and copies ran while one was open for 3% of the time, Pallas kernels for 0%

commit v1 on v0

v1 whole, which is shorter than its diff:
```python
import jax
import jax.numpy as jnp
from jax import lax
from jax.experimental import pallas as pl
from jax.experimental.pallas import tpu as pltpu
from jax.sharding import PartitionSpec as P

TILE = 128
NW_DEV = 2
TILE_DEV = 8
SRC = 1024
PAIRS = 16
REACH = 2
COLS = 512
HOMES = 16
PART = COLS // HOMES
HALF = SRC // 2
SPAN = (2 * REACH + 1) * SRC


def from_behind(value, axis, steps):
    count = lax.axis_size(axis)
    initial, last = (max(0, -steps), min(count, count - steps))
    return lax.ppermute(value, axis, [(source, source + steps) for source in range(initial, last)])


def split(value):
    high = value.astype(jnp.bfloat16)
    return high, (value - high.astype(jnp.float32)).astype(jnp.bfloat16)


def dot(a, b):
    return jnp.dot(a, b, preferred_element_type=jnp.float32)


def window_plan(tile_sector, term_charge, tiles_of, terms_of):
    count_tiles = tile_sector.shape[0]
    labels = jnp.arange(count_tiles, dtype=jnp.int32)
    source = tile_sector[tiles_of] + term_charge[terms_of]
    sectors = tile_sector[count_tiles - 1] + 1
    usable = (source >= 0) & (source < sectors)
    clipped = jnp.clip(source, 0, count_tiles - 1)
    starts = jnp.sum((tile_sector[None, :] < clipped[:, None]).astype(jnp.int32), axis=1)
    widths = jnp.sum((tile_sector[None, :] == clipped[:, None]).astype(jnp.int32), axis=1)
    return starts, jnp.where(usable, widths * TILE, 0)


def left_kernel(plan, own, m0, m1, m2, m3, s0, s1, s2, s3, block, out, high, low):
    @pl.when(pl.program_id(0) == 0)
    def _():
        core = plan[2, 0]
        for spot, (mine, swapped) in zip((0, 1, 3, 4), ((m0, s0), (m1, s1), (m2, s2), (m3, s3))):
            for value, side in ((mine, core), (swapped, 1 - core)):
                rows = pl.ds(pl.multiple_of(spot * SRC + side * HALF, HALF), HALF)
                high[rows, :], low[rows, :] = split(value[...])
        rows = pl.ds(REACH * SRC, SRC)
        high[rows, :], low[rows, :] = split(own[...])

    k = pl.program_id(0)
    live = plan[1, k]
    rows = pl.ds(pl.multiple_of(plan[0, k] * TILE, TILE), SRC)
    columns = lax.broadcasted_iota(jnp.int32, (TILE, SRC), 1)
    b_high, b_low = split(jnp.where(columns < live, block[0], 0.0))
    both = dot(jnp.concatenate([b_high, b_low], axis=0), high[rows, :])
    left = both[:TILE] + both[TILE:] + dot(b_high, low[rows, :])
    out[...] = left.T.reshape(HOMES, 1, PART, TILE)


def left_products(plan, own, mine, swapped, blocks):
    whole = pl.BlockSpec((SRC, COLS), lambda k, plan: (0, 0))
    part = pl.BlockSpec((HALF, COLS), lambda k, plan: (0, 0))
    return pl.pallas_call(
        left_kernel,
        grid_spec=pltpu.PrefetchScalarGridSpec(
            num_scalar_prefetch=1,
            grid=(PAIRS,),
            in_specs=[whole] + [part] * 8 + [pl.BlockSpec((1, TILE, SRC), lambda k, plan: (k, 0, 0))],
            out_specs=pl.BlockSpec((HOMES, 1, PART, TILE), lambda k, plan: (0, k, 0, 0)),
            scratch_shapes=[pltpu.VMEM((SPAN, COLS), jnp.bfloat16), pltpu.VMEM((SPAN, COLS), jnp.bfloat16)],
        ),
        out_shape=jax.ShapeDtypeStruct((HOMES, PAIRS, PART, TILE), jnp.float32),
        name="left_products",
    )(plan, own, *mine, *swapped, blocks)


def right_kernel(home, parts, right, out, r_high, r_low, stack):
    tile = pl.program_id(0)

    @pl.when(tile == 0)
    def _():
        r_high[...], r_low[...] = split(right[...].T)

    for w in range(HOMES * NW_DEV):
        k = tile * NW_DEV + w % NW_DEV
        stack[w * PART:(w + 1) * PART, :] = parts[home[w // NW_DEV, k], k]
    high, low = split(stack[...])
    total = dot(r_high[...], high) + dot(r_low[...], high) + dot(r_high[...], low)
    out[...] = total


def right_products(home, parts, right):
    depth = HOMES * NW_DEV * PART
    return pl.pallas_call(
        right_kernel,
        grid_spec=pltpu.PrefetchScalarGridSpec(
            num_scalar_prefetch=1,
            grid=(TILE_DEV,),
            in_specs=[
                pl.BlockSpec((HOMES, PAIRS, PART, TILE), lambda t, home: (0, 0, 0, 0)),
                pl.BlockSpec((depth, COLS), lambda t, home: (0, 0)),
            ],
            out_specs=pl.BlockSpec((COLS, TILE), lambda t, home: (0, t)),
            scratch_shapes=[
                pltpu.VMEM((COLS, depth), jnp.bfloat16),
                pltpu.VMEM((COLS, depth), jnp.bfloat16),
                pltpu.VMEM((depth, TILE), jnp.float32),
            ],
        ),
        out_shape=jax.ShapeDtypeStruct((COLS, TILE_DEV * TILE), jnp.float32),
        name="right_products",
    )(home, parts, right)


def exchange(value):
    return lax.all_to_all(value, "bulk", split_axis=0, concat_axis=0, tiled=True)


def on_device(wavefunction, env_blocks, right_env, tile_sector, term_charge, block_home):
    here = lax.axis_index("bulk")
    column = lax.axis_index("wide")
    core = here % 2
    right = exchange(right_env.reshape(NW_DEV, HOMES, PART, COLS).transpose(1, 0, 2, 3))
    right = right.reshape(HOMES * NW_DEV * PART, COLS)

    half = lax.dynamic_slice(wavefunction, (core * HALF, jnp.int32(0)), (HALF, COLS))
    mine = [from_behind(half, "wide", offset) for offset in (2, 1, -1, -2)]
    pairs = [(index, index ^ 1) for index in range(HOMES)]
    swapped = [lax.ppermute(value, "bulk", pairs) for value in mine]

    pair_ids = jnp.arange(PAIRS, dtype=jnp.int32)
    homes = jnp.arange(HOMES, dtype=jnp.int32)
    owner = jnp.sum(homes[:, None] * (block_home == here).astype(jnp.int32), axis=0)
    first_tile, live_rows = window_plan(
        tile_sector, term_charge, column * TILE_DEV + pair_ids // NW_DEV, owner * NW_DEV + pair_ids % NW_DEV
    )
    first = jnp.clip(first_tile - (column - REACH) * TILE_DEV, 0, SPAN // TILE - TILE_DEV)
    plan = jnp.stack([first, live_rows, jnp.full((PAIRS,), core, jnp.int32)])

    parts = exchange(left_products(plan, wavefunction, mine, swapped, env_blocks))
    partial = right_products(block_home, parts, right)
    pieces = exchange(partial.reshape(HOMES, PART, TILE_DEV * TILE))
    return jnp.sum(pieces, axis=0).T


def solution(mesh):
    return jax.shard_map(
        on_device,
        mesh=mesh,
        in_specs=(P("wide", None), P("bulk", "wide", None), P("bulk", None, None), P(), P(), P()),
        out_specs=P("wide", "bulk"),
        check_vma=False,
    )
```

time: 702 us -> 285 us (0.41)
  waiting for transfers between devices: 386 us -> 59.6 us
  blocking collectives: 0 us -> 157 us
  matrix products: 103 us -> 0 us
  local copies, waits for them, and re-layouts: 77.5 us -> 7.46 us
  loops' own time: 62.2 us -> 0 us
  Pallas kernels: 0 us -> 34.8 us
  other arithmetic: 28.6 us -> 1.68 us
  between operations: 14.2 us -> 0.79 us
    all_to_all x1, waiting for transfers between devices: 256 us -> 0.01 us  [exchange(): lax.all_to_all(value, 'bulk', split_axis=0, concat_axis=0, tiled=True)]
    all_to_all x0 -> x2, blocking collectives: none -> 157 us  [exchange(): lax.all_to_all(value, 'bulk', split_axis=0, concat_axis=0, tiled=True)]
    dot_general x32 -> x0, matrix products: 103 us -> none  [the longest x16 64.8 us: contract_left(): jnp.dot(env_block, window, precision=precise, preferred_element_type=jnp....]
    another operation x2 -> x0, loops' own time: 62.2 us -> none  [the longest x1 32.5 us: on_device(): left_parts = lax.map(contract_left, (blocks, first_row, live_rows))]
    reduce_scatter x1 -> x0, waiting for transfers between devices: 56.7 us -> none  [on_device(): return lax.psum_scatter(summed, 'bulk', scatter_dimension=1, tiled=True)]
    pallas_call x0 -> x2, Pallas kernels: none -> 34.8 us  [the longest x1 21.5 us: left_products(): pl.pallas_call(left_kernel, grid_spec=pltpu.PrefetchScalarGridSpec(num_sc...]
    dynamic_slice x48 -> x1, local copies, waits for them, and re-layouts: 30.2 us -> 2.27 us  [on_device(): lax.dynamic_slice(wavefunction, (core * HALF, jnp.int32(0)), (HALF, COLS))]
    gather x4 -> x0, local copies, waits for them, and re-layouts: 22.9 us -> none  [the longest x1 11.5 us: on_device(): jnp.take(env_blocks, pick_index.reshape(-1), axis=0)]
  transfers between devices with their start and end apart: 6 -> 9, of which waited for: 4 -> 5; matrix products, arithmetic and copies ran while one was open for 3% -> 2% of each run, Pallas kernels for 0% -> 8%
where the time goes in v1:
time: 285 us; the launch traced here: 284 us
  blocking collectives  157 us (55%)
  waiting for transfers between devices  59.6 us (21%)
  Pallas kernels  34.8 us (12%)
  starting transfers between devices  23 us (8%)
  local copies, waits for them, and re-layouts  7.46 us (3%)
    all_to_all x2, blocking collectives, exchange(): lax.all_to_all(value, 'bulk', split_axis=0, concat_axis=0, tiled=True)  157 us
    ppermute x4, waiting for transfers between devices, from_behind(): lax.ppermute(value, axis, [(source, source + steps) for source in range(i...  58.5 us
    pallas_call x1, Pallas kernels, left_products(): pl.pallas_call(left_kernel, grid_spec=pltpu.PrefetchScalarGridSpec(num_sc...  21.5 us
    pallas_call x1, Pallas kernels, right_products(): pl.pallas_call(right_kernel, grid_spec=pltpu.PrefetchScalarGridSpec(num_s...  13.3 us
    ppermute x4, starting transfers between devices, from_behind(): lax.ppermute(value, axis, [(source, source + steps) for source in range(i...  9.78 us
    all_to_all x1, starting transfers between devices, exchange(): lax.all_to_all(value, 'bulk', split_axis=0, concat_axis=0, tiled=True)  9.15 us
  transfers between devices with their start and end apart: 9, of which 5 were waited for; matrix products, arithmetic and copies ran while one was open for 2% of the time, Pallas kernels for 8%

profile of v1, /device:TPU:29, one launch (start us, length us, event | category | flops | bytes accessed | tf_op | source)
XLA Modules:
  0.0 284.4 jit_solution(5390141043220394551)
XLA Ops:
  0.0 3.2 %copy.11 = f32[2,16,32,512]{3,2,0,1:T(8,128)} copy(f32[2,16,32,512]{3,2,1,0:T(8,128)} %bitcast.22) | data formatting | bytes 4194304 | tf_op jit(solution)/shard_map/reshape | solution.py:132
  3.2 9.2 %all-to-all-start.1 = ((f32[16,2,32,512]{3,2,1,0:T(8,128)}), f32[16,2,32,512]{3,2,1,0:T(8,128)S(1)}, u32[]{:S(2)}, u32[]{:S(2)}) async-start(f32[16,2,32,512]{3,2,1,0:T(8,128)} %bitcast.21), calls=%async_computation.1 | async-start | bytes 4194304 | tf_op jit(solution)/shard_map/all_to_all | solution.py:125
  12.4 0.0 copy-start.4
  12.4 2.3 constant_dynamic-slice_fusion
  14.7 2.2 collective-permute-start.3
  16.9 3.9 %collective-permute-start.2 = (f32[512,512]{1,0:T(8,128)}, f32[512,512]{1,0:T(8,128)}, u32[]{:S(2)}, u32[]{:S(2)}) collective-permute-start(f32[512,512]{1,0:T(8,128)} %constant_dynamic-slice_fusion), channel_id=1, source_target_pairs={{1,0},{2,1},{3,2},{4,3},{5,4},{6,5},{7,6},{8,7},{9,8},{10,9},{11,1... | collective-permute-start | bytes 3145736 | tf_op jit(solution)/shard_map/ppermute | solution.py:24
  20.8 2.4 collective-permute-start.1
  23.2 1.3 collective-permute-start
  24.5 0.6 slice.3
  25.1 0.1 pad.2.clone
  25.2 0.7 gather_fusion
  26.5 13.0 %collective-permute-done.3.m3 = f32[512,512]{1,0:T(8,128)S(1)} collective-permute-done((f32[512,512]{1,0:T(8,128)}, f32[512,512]{1,0:T(8,128)S(1)}, u32[]{:S(2)}, u32[]{:S(2)}) %collective-permute-start.3) | collective-permute-done | bytes 1048608 | tf_op jit(solution)/shard_map/ppermute | solution.py:24
  39.5 1.5 collective-permute-start.7
  41.0 23.5 %collective-permute-done.2.m2 = f32[512,512]{1,0:T(8,128)} collective-permute-done((f32[512,512]{1,0:T(8,128)}, f32[512,512]{1,0:T(8,128)}, u32[]{:S(2)}, u32[]{:S(2)}) %collective-permute-start.2) | collective-permute-done | bytes 1048608 | tf_op jit(solution)/shard_map/ppermute | solution.py:24
  64.6 1.0 collective-permute-start.6
  65.5 1.0 collective-permute-done.1.m1
  66.5 0.6 collective-permute-start.5
  67.1 21.0 %collective-permute-done.m0 = f32[512,512]{1,0:T(8,128)} collective-permute-done((f32[512,512]{1,0:T(8,128)}, f32[512,512]{1,0:T(8,128)}, u32[]{:S(2)}, u32[]{:S(2)}) %collective-permute-start) | collective-permute-done | bytes 1048608 | tf_op jit(solution)/shard_map/ppermute | solution.py:24
  88.1 1.0 collective-permute-start.4
  89.1 0.7 gather_fusion.1
  89.8 0.2 convert_reduce_fusion.1
  90.0 0.6 add_add_fusion.plan
  90.6 0.0 collective-permute-done.7.s3
  90.7 0.0 collective-permute-done.6.s2
  90.7 0.0 collective-permute-done.5.s1
  90.7 1.1 collective-permute-done.4.s0
  91.7 21.5 %left_products.1 = f32[16,16,32,128]{3,2,1,0:T(8,128)} custom-call(s32[3,16]{1,0:T(4,128)} %add_add_fusion.plan, f32[1024,512]{1,0:T(8,128)} %own.1, f32[512,512]{1,0:T(8,128)} %collective-permute-done.m0, f32[512,512]{1,0:T(8,128)} %collective-permute-done.1.m1, f32[512,512]{1,0:T(8,128)} %collective-permute-done.2.m2, f32[512,512]{1,0:T(8,128)} %copy-done.3, ...), custom_call_target="tpu_custom_call" | custom-call | tf_op jit(solution)/shard_map/left_products/pallas_call | solution.py:72
  113.2 0.0 all-to-all-done.1
  113.2 103.2 %all_to_all.15.parts = f32[16,16,32,128]{3,2,1,0:T(8,128)} all-to-all(f32[16,16,32,128]{3,2,1,0:T(8,128)} %left_products.1), channel_id=1, replica_groups=mesh['bulk'=16,'wide'=16] {'bulk'}, dimensions={0} | all-to-all | bytes 8388608 | tf_op jit(solution)/shard_map/all_to_all | solution.py:125
  216.4 13.3 %right_products.1 = f32[512,1024]{1,0:T(8,128)} custom-call(s32[16,16]{1,0:T(8,128)} %home.1, f32[16,16,32,128]{3,2,1,0:T(8,128)} %all_to_all.15.parts, f32[1024,512]{1,0:T(8,128)} %bitcast.19), custom_call_target="tpu_custom_call" | custom-call | tf_op jit(solution)/shard_map/right_products/pallas_call | solution.py:103
  229.7 53.9 %all_to_all.16 = f32[16,32,1024]{2,1,0:T(8,128)S(1)} all-to-all(f32[16,32,1024]{2,1,0:T(8,128)} %bitcast.20), channel_id=1, replica_groups=mesh['bulk'=16,'wide'=16] {'bulk'}, dimensions={0} | all-to-all | bytes 4194304 | tf_op jit(solution)/shard_map/all_to_all | solution.py:125
  283.6 0.8 reduce_sum.39
  (16 shorter events, 0.1 us)
Async XLA Ops:
  0.0 89.1 %copy-start = (s32[32]{0:T(128)S(1)}, s32[32]{0:T(128)}, u32[]{:S(2)}) copy-start(s32[32]{0:T(128)} %param.10) | copy-start | bytes 388
  3.2 110.0 %all-to-all-start.1 = ((f32[16,2,32,512]{3,2,1,0:T(8,128)}), f32[16,2,32,512]{3,2,1,0:T(8,128)S(1)}, u32[]{:S(2)}, u32[]{:S(2)}) async-start(f32[16,2,32,512]{3,2,1,0:T(8,128)} %bitcast.21), calls=%async_computation.1 | async-start | bytes 4194304 | tf_op jit(solution)/shard_map/all_to_all | solution.py:125
  12.4 12.1 %copy-start.1 = (s32[128]{0:T(128)S(1)}, s32[128]{0:T(128)}, u32[]{:S(2)}) copy-start(s32[128]{0:T(128)} %param.9) | copy-start | bytes 1540
  12.4 14.1 %copy-start.4 = (s32[16,16]{1,0:T(8,128)S(1)}, s32[16,16]{1,0:T(8,128)}, u32[]{:S(2)}) copy-start(s32[16,16]{1,0:T(8,128)} %home.1) | copy-start | bytes 3076
  14.7 24.8 %collective-permute-start.3 = (f32[512,512]{1,0:T(8,128)}, f32[512,512]{1,0:T(8,128)S(1)}, u32[]{:S(2)}, u32[]{:S(2)}) collective-permute-start(f32[512,512]{1,0:T(8,128)} %constant_dynamic-slice_fusion), channel_id=1, source_target_pairs={{2,0},{3,1},{4,2},{5,3},{6,4},{7,5},{8,6},{9,7},{10,8},{11,9},{12,... | collective-permute-start | bytes 3145736 | tf_op jit(solution)/shard_map/ppermute | solution.py:24
  16.9 47.7 %collective-permute-start.2 = (f32[512,512]{1,0:T(8,128)}, f32[512,512]{1,0:T(8,128)}, u32[]{:S(2)}, u32[]{:S(2)}) collective-permute-start(f32[512,512]{1,0:T(8,128)} %constant_dynamic-slice_fusion), channel_id=1, source_target_pairs={{1,0},{2,1},{3,2},{4,3},{5,4},{6,5},{7,6},{8,7},{9,8},{10,9},{11,1... | collective-permute-start | bytes 3145736 | tf_op jit(solution)/shard_map/ppermute | solution.py:24
  20.8 45.7 %collective-permute-start.1 = (f32[512,512]{1,0:T(8,128)}, f32[512,512]{1,0:T(8,128)}, u32[]{:S(2)}, u32[]{:S(2)}) collective-permute-start(f32[512,512]{1,0:T(8,128)} %constant_dynamic-slice_fusion), channel_id=1, source_target_pairs={{0,1},{1,2},{2,3},{3,4},{4,5},{5,6},{6,7},{7,8},{8,9},{9,10},{10,1... | collective-permute-start | bytes 3145736 | tf_op jit(solution)/shard_map/ppermute | solution.py:24
  23.2 65.0 %collective-permute-start = (f32[512,512]{1,0:T(8,128)}, f32[512,512]{1,0:T(8,128)}, u32[]{:S(2)}, u32[]{:S(2)}) collective-permute-start(f32[512,512]{1,0:T(8,128)} %constant_dynamic-slice_fusion), channel_id=1, source_target_pairs={{0,2},{1,3},{2,4},{3,5},{4,6},{5,7},{6,8},{7,9},{8,10},{9,11},{10,... | collective-permute-start | bytes 3145736 | tf_op jit(solution)/shard_map/ppermute | solution.py:24
  39.5 52.2 %copy-start.3 = (f32[512,512]{1,0:T(8,128)}, f32[512,512]{1,0:T(8,128)S(1)}, u32[]{:S(2)}) copy-start(f32[512,512]{1,0:T(8,128)S(1)} %collective-permute-done.3.m3) | copy-start | bytes 3145732
  39.5 51.1 %collective-permute-start.7 = (f32[512,512]{1,0:T(8,128)S(1)}, f32[512,512]{1,0:T(8,128)}, u32[]{:S(2)}, u32[]{:S(2)}) collective-permute-start(f32[512,512]{1,0:T(8,128)S(1)} %collective-permute-done.3.m3), channel_id=1, source_target_pairs={{0,16},{16,0},{32,48},{48,32},{64,80},{80,64},{96,112},{112,96},{1... | collective-permute-start | bytes 3145736 | tf_op jit(solution)/shard_map/ppermute | solution.py:138
  64.6 26.1 %collective-permute-start.6 = (f32[512,512]{1,0:T(8,128)}, f32[512,512]{1,0:T(8,128)}, u32[]{:S(2)}, u32[]{:S(2)}) collective-permute-start(f32[512,512]{1,0:T(8,128)} %collective-permute-done.2.m2), channel_id=1, source_target_pairs={{0,16},{16,0},{32,48},{48,32},{64,80},{80,64},{96,112},{112,96},{1... | collective-permute-start | bytes 3145736 | tf_op jit(solution)/shard_map/ppermute | solution.py:138
  66.5 24.1 %collective-permute-start.5 = (f32[512,512]{1,0:T(8,128)}, f32[512,512]{1,0:T(8,128)}, u32[]{:S(2)}, u32[]{:S(2)}) collective-permute-start(f32[512,512]{1,0:T(8,128)} %collective-permute-done.1.m1), channel_id=1, source_target_pairs={{0,16},{16,0},{32,48},{48,32},{64,80},{80,64},{96,112},{112,96},{1... | collective-permute-start | bytes 3145736 | tf_op jit(solution)/shard_map/ppermute | solution.py:138
  88.1 3.6 %collective-permute-start.4 = (f32[512,512]{1,0:T(8,128)}, f32[512,512]{1,0:T(8,128)}, u32[]{:S(2)}, u32[]{:S(2)}) collective-permute-start(f32[512,512]{1,0:T(8,128)} %collective-permute-done.m0), channel_id=1, source_target_pairs={{0,16},{16,0},{32,48},{48,32},{64,80},{80,64},{96,112},{112,96},{1... | collective-permute-start | bytes 3145736 | tf_op jit(solution)/shard_map/ppermute | solution.py:138
  113.2 103.2 %copy-start.2 = (f32[16,2,32,512]{3,2,1,0:T(8,128)}, f32[16,2,32,512]{3,2,1,0:T(8,128)S(1)}, u32[]{:S(2)}) copy-start(f32[16,2,32,512]{3,2,1,0:T(8,128)S(1)} %all-to-all-done.1) | copy-start | bytes 6291460
